TPU v7x, 256 devices: a whole 4x4x8 slice. The times are simulated.
256 devices in a mesh: dp: 8 (over z_lo, x), ctx: 32 (over z_hi, y, core).
Axes of the slice: x: 4, y: 4, z: 8 (z_hi: 4, z_lo: 2; z = z_hi * 2 + z_lo), core: 2. Of those that a mesh axis runs over, the one named last changes fastest.
Arguments:
- tokens: bfloat16 [8, 4096, 4096], P('dp', 'ctx'), may hold values from -6 to 6
- proj_weight: bfloat16 [4096, 512], P('dp'), may hold values from -0.09375 to 0.09375
- values: bfloat16 [8, 4096, 2048], P('dp', 'ctx'), may hold values from -60 to 60
- grad_out: bfloat16 [8, 4096, 2048], P('dp', 'ctx'), may hold values from -6 to 6
Outputs:
- attended: bfloat16 [8, 4096, 2048], P('dp', 'ctx')
- grad_tokens: bfloat16 [8, 4096, 4096], P('dp', 'ctx')
- grad_values: bfloat16 [8, 4096, 2048], P('dp', 'ctx')
- grad_proj: float32 [4096, 512], P(('dp', 'ctx'))
All inputs are finite; a program needn't handle non-finite values.
Results may differ from a plain program's by a relative error of at most 0.0049.
Values may be sent and summed in bfloat16 or wider, within the bound.
A program may use at most 192 MiB of HBM per device.

v0:
```python
import jax
import jax.numpy as jnp
from jax import lax
from jax.sharding import PartitionSpec as P

H = 16
F = 16
DH = 128
HIGHEST = lax.Precision.HIGHEST
QUAD_SCALE = 0.17677669529663687
EPSILON = 1e-05


def features(inputs):
    count_heads, count_rows, count_feat = inputs.shape
    linear = jnp.swapaxes(inputs, 1, 2) * 0.5
    square = (inputs[:, :, :, None] * inputs[:, :, None, :]).reshape(
        count_heads, count_rows, count_feat * count_feat
    )
    square = jnp.swapaxes(square, 1, 2) * QUAD_SCALE
    constant_row = jnp.ones((count_heads, 1, count_rows), inputs.dtype)
    return jnp.concatenate([constant_row, linear, square], axis=1)


def block_kernel(query_part, key_part):
    count_rows = query_part.shape[1]
    causal = lax.broadcasted_iota(jnp.int32, (count_rows, count_rows), 0) >= lax.broadcasted_iota(
        jnp.int32, (count_rows, count_rows), 1
    )
    scores = jnp.einsum("htf,hsf->hts", query_part, key_part, precision=HIGHEST) * 0.25
    kernel = jnp.where(causal, 1.0 + scores + 0.5 * scores * scores, 0.0)
    return (causal, scores, kernel)


def normalize(numerator):
    inv_rms = lax.rsqrt(jnp.mean(numerator * numerator, axis=-1, keepdims=True) + EPSILON)
    return (inv_rms, numerator * inv_rms)


def grad_normalize(inv_rms, normed, upstream):
    return inv_rms * (upstream - normed * jnp.mean(normed * upstream, axis=-1, keepdims=True))


def local_backward(
    query_part,
    key_part,
    value_part,
    grad_num,
    causal,
    scores,
    kernel,
    pull_query,
    pull_key,
    feat_key,
    prefix,
    suffix,
):
    mixing = jnp.where(
        causal, jnp.einsum("htd,hsd->hts", grad_num, value_part, precision=HIGHEST), 0.0
    )
    slope = mixing * (1.0 + scores)
    grad_query = jnp.einsum("hts,hsf->htf", slope, key_part, precision=HIGHEST) * 0.25
    grad_key = jnp.einsum("hts,htf->hsf", slope, query_part, precision=HIGHEST) * 0.25
    grad_query = (
        grad_query + pull_query(jnp.einsum("hed,htd->het", prefix, grad_num, precision=HIGHEST))[0]
    )
    grad_key = (
        grad_key + pull_key(jnp.einsum("hed,htd->het", suffix, value_part, precision=HIGHEST))[0]
    )
    grad_value = jnp.einsum("hts,htd->hsd", kernel, grad_num, precision=HIGHEST)
    grad_value = grad_value + jnp.einsum("het,hed->htd", feat_key, suffix, precision=HIGHEST)
    return (grad_query, grad_key, grad_value)


def split_heads(matrix, size):
    return jnp.swapaxes(matrix.reshape(matrix.shape[0], -1, size), 0, 1)


def merge_heads(blocked):
    return jnp.swapaxes(blocked, 0, 1).reshape(blocked.shape[1], -1)


def local(tokens, proj_weight, values, grad_out):
    token_rows = tokens[0]
    query_cols = H * F
    projected = jnp.dot(
        token_rows,
        lax.all_gather(proj_weight, "dp", axis=0, tiled=True),
        preferred_element_type=jnp.float32,
    )
    query_part = split_heads(projected[:, :query_cols], F)
    key_part = split_heads(projected[:, query_cols:], F)
    value_part = split_heads(values[0].astype(jnp.float32), DH)
    upstream = split_heads(grad_out[0].astype(jnp.float32), DH)
    feat_query, pull_query = jax.vjp(features, query_part)
    feat_key, pull_key = jax.vjp(features, key_part)
    local_term = jnp.einsum("het,htd->hed", feat_key, value_part, precision=HIGHEST)
    columns_in = lax.all_to_all(
        local_term.reshape(1, -1), "ctx", split_axis=1, concat_axis=0, tiled=True
    )
    shifted = jnp.concatenate([jnp.zeros_like(columns_in[:1]), columns_in[:-1]], axis=0)
    running = jnp.cumsum(shifted, axis=0)
    prefix = lax.all_to_all(running, "ctx", split_axis=0, concat_axis=1, tiled=True).reshape(
        local_term.shape
    )
    causal, scores, kernel = block_kernel(query_part, key_part)
    numerator = jnp.einsum("hts,hsd->htd", kernel, value_part, precision=HIGHEST)
    numerator = numerator + jnp.einsum("het,hed->htd", feat_query, prefix, precision=HIGHEST)
    inv_rms, normed = normalize(numerator)
    attended = merge_heads(normed).astype(jnp.bfloat16)
    grad_num = grad_normalize(inv_rms, normed, upstream)
    carried = jnp.einsum("het,htd->hed", feat_query, grad_num, precision=HIGHEST)
    later_in = lax.all_to_all(
        carried.reshape(1, -1), "ctx", split_axis=1, concat_axis=0, tiled=True
    )
    later_shift = jnp.concatenate([later_in[1:], jnp.zeros_like(later_in[:1])], axis=0)
    later_running = jnp.cumsum(later_shift[::-1], axis=0)[::-1]
    suffix = lax.all_to_all(later_running, "ctx", split_axis=0, concat_axis=1, tiled=True).reshape(
        carried.shape
    )
    grad_query, grad_key, grad_value = local_backward(
        query_part,
        key_part,
        value_part,
        grad_num,
        causal,
        scores,
        kernel,
        pull_query,
        pull_key,
        feat_key,
        prefix,
        suffix,
    )
    grad_proj_rows = jnp.concatenate(
        [merge_heads(grad_query), merge_heads(grad_key)], axis=1
    ).astype(jnp.bfloat16)
    grad_tokens = lax.dot_general(
        grad_proj_rows,
        lax.all_gather(proj_weight, "dp", axis=0, tiled=True),
        (((1,), (1,)), ((), ())),
        preferred_element_type=jnp.float32,
    ).astype(jnp.bfloat16)
    grad_proj = lax.psum_scatter(
        lax.dot_general(
            token_rows, grad_proj_rows, (((0,), (0,)), ((), ())), preferred_element_type=jnp.float32
        ),
        ("dp", "ctx"),
        scatter_dimension=0,
        tiled=True,
    )
    grad_values = merge_heads(grad_value).astype(jnp.bfloat16)
    return (attended[None], grad_tokens[None], grad_values[None], grad_proj)


def solution(mesh):
    return jax.shard_map(
        local,
        mesh=mesh,
        in_specs=(P("dp", "ctx", None), P("dp", None), P("dp", "ctx", None), P("dp", "ctx", None)),
        out_specs=(
            P("dp", "ctx", None),
            P("dp", "ctx", None),
            P("dp", "ctx", None),
            P(("dp", "ctx"), None),
        ),
        check_vma=False,
    )
```

profile of v0, /device:TPU:32, one launch (start us, length us, event | category | flops | bytes accessed | tf_op | source)
XLA Modules:
  0.0 2036.4 jit_solution(6238759362847132041)
XLA Ops:
  7.2 0.7 all-gather.2.cloned.1.call-update
  7.9 1.1 copy.57
  9.1 57.5 %all-gather.2.cloned.1.call-done = bf16[4096,512]{1,0:T(8,128)(2,1)} async-done(((bf16[512,512]{1,0:T(8,128)(2,1)}), bf16[4096,512]{1,0:T(8,128)(2,1)}) %all-gather.2.cloned.1.call-update) | async-done | bytes 4194320 | tf_op jit(solution)/shard_map/all_gather | solution.py:88
  66.6 2.9 fusion.20
  69.5 0.7 fusion.59
  70.3 0.3 multiply_multiply_fusion
  70.6 0.3 copy-done.14
  70.9 1.0 copy-done.3
  71.9 3.5 fusion.3
  75.4 4.0 all_to_all.45
  79.4 65.7 %all_to_all.51 = f32[1,32,17472]{2,0,1:T(1,128)S(1)} all-to-all(f32[1,32,17472]{2,0,1:T(1,128)S(1)} %all_to_all.45), channel_id=1, replica_groups=mesh['dp'=8,'ctx'=32] {'ctx'}, dimensions={1} | all-to-all | bytes 4472832 | tf_op jit(solution)/shard_map/all_to_all | solution.py:98
  145.1 2.6 fusion.1
  147.6 4.2 all-to-all-start.1
  151.9 2.2 copy.39
  154.1 1.7 copy.34
  155.8 1.6 multiply_bitcast_fusion.1
  157.4 3.7 fusion.60
  161.0 2.6 multiply_multiply_fusion.1
  163.6 43.2 %all-to-all-done.1 = f32[32,1,17472]{2,1,0:T(1,128)S(1)} async-done(((f32[32,1,17472]{2,1,0:T(1,128)}), f32[32,1,17472]{2,1,0:T(1,128)S(1)}, u32[]{:S(2)}, u32[]{:S(2)}) %all-to-all-start.1) | async-done | bytes 2236448 | tf_op jit(solution)/shard_map/all_to_all | solution.py:103
  206.8 7.3 reduce
  214.1 2.4 reshape.141
  216.6 7.7 fusion.5
  224.4 1.4 multiply_reduce_fusion.5
  225.8 0.2 multiply_reduce_fusion.4
  226.0 0.8 copy-done.6
  226.8 0.2 subtract_multiply_fusion
  227.0 0.7 copy-done.2
  227.7 5.2 fusion.4
  233.0 5.1 all_to_all.46
  238.1 60.0 %all_to_all.52 = f32[1,32,17472]{2,0,1:T(1,128)S(1)} all-to-all(f32[1,32,17472]{2,0,1:T(1,128)} %all_to_all.46), channel_id=1, replica_groups=mesh['dp'=8,'ctx'=32] {'ctx'}, dimensions={1} | all-to-all | bytes 4472832 | tf_op jit(solution)/shard_map/all_to_all | solution.py:113
  298.0 0.2 slice.24
  298.2 0.2 copy.75
  298.4 1.6 concatenate.16
  299.9 60.9 %rev.6 = f32[32,17472]{1,0:T(8,128)} reverse(f32[32,17472]{1,0:T(8,128)} %concatenate.16), dimensions={0} | reverse | bytes 4472832 | tf_op jit(solution)/shard_map/rev | solution.py:117
  360.8 4.9 reduce_window_sum.21
  365.7 60.9 %rev.7 = f32[32,17472]{1,0:T(8,128)} reverse(f32[32,17472]{1,0:T(8,128)} %reduce_window_sum.21), dimensions={0} | reverse | bytes 4472832 | tf_op jit(solution)/shard_map/rev | solution.py:117
  426.6 5.3 copy.44
  431.9 4.8 all-to-all-start.3
  436.7 0.2 reduce-scatter.4.cloned.1.call-start
  437.0 5.5 fusion.61
  442.5 0.3 slice_multiply_fusion.1
  442.8 0.6 copy-done.13
  443.4 1.1 multiply_reduce_fusion.2
  444.4 0.2 copy-done.5
  444.7 1.0 fusion.6
  445.8 1.0 copy-done.11
  446.7 1.7 fusion.17
  448.5 42.8 %all-to-all-done.3 = f32[32,1,17472]{2,1,0:T(1,128)} async-done(((f32[32,1,17472]{2,1,0:T(1,128)}), f32[32,1,17472]{2,1,0:T(1,128)}, u32[]{:S(2)}, u32[]{:S(2)}) %all-to-all-start.3) | async-done | bytes 2236448 | tf_op jit(solution)/shard_map/all_to_all | solution.py:118
  491.3 8.6 reduce.1
  499.8 3.2 reshape.144
  503.0 3.8 fusion.25
  506.8 0.3 slice_multiply_fusion
  507.1 1.1 multiply_reduce_fusion
  508.1 0.2 copy-done.12
  508.3 1.0 fusion.16
  509.3 4.5 convolution_bitcast_fusion
  513.8 9.2 copy.54
  523.0 2.2 fusion.18
  525.2 2.0 copy.45
  527.3 7.6 fusion.2
  534.8 2.1 fusion.7
  537.0 2.0 copy.46
  539.0 4.7 fusion
  543.7 1485.6 %reduce-scatter.4.cloned.1.call-done = f32[16,512]{1,0:T(8,128)} async-done(((f32[4096,512]{1,0:T(8,128)}), f32[16,512]{1,0:T(8,128)}) %reduce-scatter.4.cloned.1.call-update) | async-done | bytes 32784
  (34 shorter events, 0.4 us)
Async XLA Ops:
  7.2 59.4 %copy-start = (bf16[1,128,4096]{2,1,0:T(8,128)(2,1)S(1)}, bf16[1,128,4096]{2,1,0:T(8,128)(2,1)}, u32[]{:S(2)}) copy-start(bf16[1,128,4096]{2,1,0:T(8,128)(2,1)} %param.4) | copy-start | bytes 3145732
  7.2 59.4 %all-gather.2.cloned.1.call-start = ((), (), s32[]{:S(2)}) async-start(), calls=%async_computation.5 | async-start | bytes 4718592 | tf_op jit(solution)/shard_map/all_gather | solution.py:88
  9.1 61.5 %copy-start.7 = (bf16[16,8,16,128]{3,2,1,0:T(8,128)(2,1)}, bf16[16,8,16,128]{3,2,1,0:T(8,128)(2,1)S(1)}, u32[]{:S(2)}) copy-start(bf16[16,8,16,128]{3,2,1,0:T(8,128)(2,1)S(1)} %copy.57) | copy-start | bytes 1572868
  70.2 0.6 copy-start.14
  70.5 1.3 copy-start.3
  147.6 59.2 %all-to-all-start.1 = ((f32[32,1,17472]{2,1,0:T(1,128)}), f32[32,1,17472]{2,1,0:T(1,128)S(1)}, u32[]{:S(2)}, u32[]{:S(2)}) async-start(f32[32,1,17472]{2,1,0:T(1,128)} %fusion.1), calls=%async_computation.1 | async-start | bytes 4489216 | tf_op jit(solution)/shard_map/all_to_all | solution.py:103
  216.6 7.8 copy-start.1
  216.6 7.8 copy-start.4
  216.6 7.8 copy-start.8
  224.3 1.4 copy-start.10
  225.7 1.1 copy-start.6
  225.8 2.0 copy-start.2
  225.8 1.9 copy-start.16
  431.9 59.3 %all-to-all-start.3 = ((f32[32,1,17472]{2,1,0:T(1,128)}), f32[32,1,17472]{2,1,0:T(1,128)}, u32[]{:S(2)}, u32[]{:S(2)}) async-start(f32[32,1,17472]{2,1,0:T(1,128)} %copy.44), calls=%async_computation.3 | async-start | bytes 4489216 | tf_op jit(solution)/shard_map/all_to_all | solution.py:118
  436.7 1592.6 %reduce-scatter.4.cloned.1.call-start = ((), (), s32[]{:S(2)}) async-start(), calls=%async_computation.6 | async-start | bytes 8421376
  442.5 0.9 copy-start.13
  443.4 1.2 copy-start.5
  443.4 1.4 copy-start.9
  445.8 1.0 copy-start.11
  507.1 1.2 copy-start.12
  523.0 4.2 copy-start.15
Sparse Core Ops, SparseCore 0:
  9.8 56.6 all-gather.1
  523.1 1506.1 reduce-scatter.3
where the time goes:
time: 2050 us; the launch traced here: 2040 us
  waiting for transfers between devices  1630 us (80%)
  local copies, waits for them, and re-layouts  168 us (8%)
  blocking collectives  126 us (6%)
  matrix products  56.2 us (3%)
  other arithmetic  33 us (2%)
    unnamed x3, waiting for transfers between devices  1490 us
    rev x2, local copies, waits for them, and re-layouts, local(): later_running = jnp.cumsum(later_shift[::-1], axis=0)[::-1]  122 us
    all_to_all x1, blocking collectives, local(): lax.all_to_all(local_term.reshape(1, -1), 'ctx', split_axis=1, concat_axi...  65.7 us
    all_to_all x1, blocking collectives, local(): lax.all_to_all(carried.reshape(1, -1), 'ctx', split_axis=1, concat_axis=0...  60 us
    all_gather x1, waiting for transfers between devices, local(): lax.all_gather(proj_weight, 'dp', axis=0, tiled=True)  57.5 us
    all_to_all x1, waiting for transfers between devices, local(): lax.all_to_all(running, 'ctx', split_axis=0, concat_axis=1, tiled=True)  43.2 us
    all_to_all x1, waiting for transfers between devices, local(): lax.all_to_all(later_running, 'ctx', split_axis=0, concat_axis=1, tiled=T...  42.8 us
  transfers between devices with their start and end apart: 4, of which 4 were waited for; matrix products, arithmetic and copies ran while one was open for 2% of the time, Pallas kernels for 0%

commit v1 on v0

--- a/solution.py
+++ b/solution.py
@@ -85,7 +85,9 @@
     query_cols = H * F
     projected = jnp.dot(
         token_rows,
-        lax.all_gather(proj_weight, "dp", axis=0, tiled=True),
+        jnp.concatenate(
+            lax.all_to_all(jnp.stack([proj_weight] * lax.axis_size("dp")), "dp", 0, 0), axis=0
+        ),
         preferred_element_type=jnp.float32,
     )
     query_part = split_heads(projected[:, :query_cols], F)

time: 2050 us -> 2080 us (1.015)
  waiting for transfers between devices: 1630 us -> 1690 us
  blocking collectives: 126 us -> 66.3 us
    all_to_all x0 -> x2, waiting for transfers between devices: none -> 120 us  [the longest x1 72.4 us: local(): lax.all_to_all(carried.reshape(1, -1), 'ctx', split_axis=1, concat_axis=0...]
    all_to_all x1 -> x0, blocking collectives: 60 us -> none  [local(): lax.all_to_all(carried.reshape(1, -1), 'ctx', split_axis=1, concat_axis=0...]
    all_gather x1, waiting for transfers between devices: 57.5 us -> 0.01 us  [local(): lax.all_gather(proj_weight, 'dp', axis=0, tiled=True)]
  transfers between devices with their start and end apart: 4 -> 6, of which waited for: 4 -> 5; matrix products, arithmetic and copies ran while one was open for 2% -> 10% of each run, Pallas kernels for 0% -> 0%
where the time goes in v1:
time: 2080 us; the launch traced here: 2060 us
  waiting for transfers between devices  1690 us (81%)
  local copies, waits for them, and re-layouts  172 us (8%)
  blocking collectives  66.3 us (3%)
  matrix products  56.2 us (3%)
  other arithmetic  33 us (2%)
  starting transfers between devices  22.8 us (1%)
    unnamed x3, waiting for transfers between devices  1490 us
    rev x2, local copies, waits for them, and re-layouts, local(): later_running = jnp.cumsum(later_shift[::-1], axis=0)[::-1]  122 us
    all_to_all x1, waiting for transfers between devices, local(): lax.all_to_all(carried.reshape(1, -1), 'ctx', split_axis=1, concat_axis=0...  72.4 us
    all_to_all x1, blocking collectives, local(): lax.all_to_all(local_term.reshape(1, -1), 'ctx', split_axis=1, concat_axi...  66.3 us
    all_to_all x1, waiting for transfers between devices, local(): lax.all_to_all(jnp.stack([proj_weight] * lax.axis_size('dp')), 'dp', 0, 0)  47.4 us
    all_to_all x1, waiting for transfers between devices, local(): lax.all_to_all(running, 'ctx', split_axis=0, concat_axis=1, tiled=True)  43.3 us
  transfers between devices with their start and end apart: 6, of which 5 were waited for; matrix products, arithmetic and copies ran while one was open for 10% of the time, Pallas kernels for 0%

profile of v1, /device:TPU:32, one launch (start us, length us, event | category | flops | bytes accessed | tf_op | source)
XLA Modules:
  0.0 2057.5 jit_solution(18259418175108732489)
XLA Ops:
  8.0 3.5 stack.2
  11.5 6.4 all-to-all-start
  18.0 47.4 %all-to-all-done = bf16[8,512,512]{2,1,0:T(8,128)(2,1)} async-done(((bf16[8,512,512]{2,1,0:T(8,128)(2,1)}), bf16[8,512,512]{2,1,0:T(8,128)(2,1)}, u32[]{:S(2)}, u32[]{:S(2)}) %all-to-all-start) | async-done | bytes 4194336 | tf_op jit(solution)/shard_map/all_to_all | solution.py:89
  65.4 2.9 fusion.20
  68.3 0.7 fusion.59
  69.1 0.3 multiply_multiply_fusion
  69.4 0.3 copy-done.14
  69.8 1.0 copy-done.3
  70.8 3.5 fusion.3
  74.2 4.0 all_to_all.49
  78.2 66.3 %all_to_all.56 = f32[1,32,17472]{2,0,1:T(1,128)S(1)} all-to-all(f32[1,32,17472]{2,0,1:T(1,128)S(1)} %all_to_all.49), channel_id=1, replica_groups=mesh['dp'=8,'ctx'=32] {'ctx'}, dimensions={1} | all-to-all | bytes 4472832 | tf_op jit(solution)/shard_map/all_to_all | solution.py:100
  144.6 2.6 fusion.1
  147.2 4.2 all-to-all-start.2
  151.4 2.2 copy.39
  153.7 1.6 copy.34
  155.3 1.6 multiply_bitcast_fusion.1
  156.9 3.7 fusion.60
  160.6 2.6 multiply_multiply_fusion.1
  163.2 43.3 %all-to-all-done.2 = f32[32,1,17472]{2,1,0:T(1,128)S(1)} async-done(((f32[32,1,17472]{2,1,0:T(1,128)}), f32[32,1,17472]{2,1,0:T(1,128)S(1)}, u32[]{:S(2)}, u32[]{:S(2)}) %all-to-all-start.2) | async-done | bytes 2236448 | tf_op jit(solution)/shard_map/all_to_all | solution.py:105
  206.5 7.3 reduce
  213.8 2.4 reshape.147
  216.2 7.7 fusion.5
  224.0 1.4 multiply_reduce_fusion.5
  225.4 0.2 multiply_reduce_fusion.4
  225.6 0.8 copy-done.6
  226.4 0.2 subtract_multiply_fusion
  226.6 0.7 copy-done.2
  227.4 5.2 fusion.4
  232.6 5.1 all_to_all.50
  237.7 4.8 all-to-all-start.3
  242.6 0.7 all-gather.2.cloned.1.call-update
  243.3 72.4 %all-to-all-done.3 = f32[1,32,17472]{2,0,1:T(1,128)} async-done(((f32[1,32,17472]{2,0,1:T(1,128)}), f32[1,32,17472]{2,0,1:T(1,128)}, u32[]{:S(2)}, u32[]{:S(2)}) %all-to-all-start.3) | async-done | bytes 2236448 | tf_op jit(solution)/shard_map/all_to_all | solution.py:115
  315.7 1.8 slice.24
  317.5 0.2 copy.75
  317.7 1.6 concatenate.16
  319.2 61.0 %rev.6 = f32[32,17472]{1,0:T(8,128)} reverse(f32[32,17472]{1,0:T(8,128)} %concatenate.16), dimensions={0} | reverse | bytes 4472832 | tf_op jit(solution)/shard_map/rev | solution.py:119
  380.2 4.9 reduce_window_sum.21
  385.1 61.0 %rev.7 = f32[32,17472]{1,0:T(8,128)} reverse(f32[32,17472]{1,0:T(8,128)} %reduce_window_sum.21), dimensions={0} | reverse | bytes 4472832 | tf_op jit(solution)/shard_map/rev | solution.py:119
  446.0 5.4 copy.44
  451.4 7.1 all-to-all-start.4
  458.5 0.2 reduce-scatter.4.cloned.1.call-start
  458.7 5.5 fusion.61
  464.3 0.3 slice_multiply_fusion.1
  464.5 0.6 copy-done.13
  465.2 1.1 multiply_reduce_fusion.2
  466.5 1.0 fusion.6
  467.6 1.0 copy-done.11
  468.5 1.7 fusion.17
  470.3 38.0 %all-to-all-done.4 = f32[32,1,17472]{2,1,0:T(1,128)} async-done(((f32[32,1,17472]{2,1,0:T(1,128)}), f32[32,1,17472]{2,1,0:T(1,128)}, u32[]{:S(2)}, u32[]{:S(2)}) %all-to-all-start.4) | async-done | bytes 2236448 | tf_op jit(solution)/shard_map/all_to_all | solution.py:120
  508.2 8.6 reduce.1
  516.8 3.2 reshape.150
  520.0 3.8 fusion.25
  523.8 0.3 slice_multiply_fusion
  524.1 1.1 multiply_reduce_fusion
  525.3 1.0 fusion.16
  526.3 4.5 convolution_bitcast_fusion
  530.7 9.2 copy.54
  540.0 2.2 fusion.18
  542.2 2.0 copy.45
  544.3 7.6 fusion.2
  551.8 2.1 fusion.7
  554.0 2.0 copy.46
  556.0 4.7 fusion
  560.6 1489.2 %reduce-scatter.4.cloned.1.call-done = f32[16,512]{1,0:T(8,128)} async-done(((f32[4096,512]{1,0:T(8,128)}), f32[16,512]{1,0:T(8,128)}) %reduce-scatter.4.cloned.1.call-update) | async-done | bytes 32784
  (40 shorter events, 0.8 us)
Async XLA Ops:
  8.0 57.4 %copy-start = (bf16[1,128,4096]{2,1,0:T(8,128)(2,1)S(1)}, bf16[1,128,4096]{2,1,0:T(8,128)(2,1)}, u32[]{:S(2)}) copy-start(bf16[1,128,4096]{2,1,0:T(8,128)(2,1)} %param.4) | copy-start | bytes 3145732
  11.5 6.4 copy-start.17
  11.5 53.9 %all-to-all-start = ((bf16[8,512,512]{2,1,0:T(8,128)(2,1)}), bf16[8,512,512]{2,1,0:T(8,128)(2,1)}, u32[]{:S(2)}, u32[]{:S(2)}) async-start(bf16[8,512,512]{2,1,0:T(8,128)(2,1)} %stack.2), calls=%async_computation | async-start | bytes 8388608 | tf_op jit(solution)/shard_map/all_to_all | solution.py:89
  18.0 51.4 %copy-start.7 = (bf16[16,8,16,128]{3,2,1,0:T(8,128)(2,1)}, bf16[16,8,16,128]{3,2,1,0:T(8,128)(2,1)S(1)}, u32[]{:S(2)}) copy-start(bf16[16,8,16,128]{3,2,1,0:T(8,128)(2,1)S(1)} %copy.57) | copy-start | bytes 1572868
  69.1 0.7 copy-start.14
  69.4 1.4 copy-start.3
  147.2 59.3 %all-to-all-start.2 = ((f32[32,1,17472]{2,1,0:T(1,128)}), f32[32,1,17472]{2,1,0:T(1,128)S(1)}, u32[]{:S(2)}, u32[]{:S(2)}) async-start(f32[32,1,17472]{2,1,0:T(1,128)} %fusion.1), calls=%async_computation.2 | async-start | bytes 4489216 | tf_op jit(solution)/shard_map/all_to_all | solution.py:105
  216.2 7.8 copy-start.1
  216.2 7.8 copy-start.4
  216.2 7.8 copy-start.8
  224.0 1.4 copy-start.10
  225.4 1.1 copy-start.6
  225.4 2.0 copy-start.2
  225.4 1.9 copy-start.16
  237.7 78.0 %all-to-all-start.3 = ((f32[1,32,17472]{2,0,1:T(1,128)}), f32[1,32,17472]{2,0,1:T(1,128)}, u32[]{:S(2)}, u32[]{:S(2)}) async-start(f32[1,32,17472]{2,0,1:T(1,128)} %all_to_all.50), calls=%async_computation.3 | async-start | bytes 4489216 | tf_op jit(solution)/shard_map/all_to_all | solution.py:115
  242.5 313.4 %all-gather.2.cloned.1.call-start = ((), (), s32[]{:S(2)}) async-start(), calls=%async_computation.6 | async-start | bytes 4718592 | tf_op jit(solution)/shard_map/all_gather | solution.py:142
  451.4 56.8 %all-to-all-start.4 = ((f32[32,1,17472]{2,1,0:T(1,128)}), f32[32,1,17472]{2,1,0:T(1,128)}, u32[]{:S(2)}, u32[]{:S(2)}) async-start(f32[32,1,17472]{2,1,0:T(1,128)} %copy.44), calls=%async_computation.4 | async-start | bytes 4489216 | tf_op jit(solution)/shard_map/all_to_all | solution.py:120
  458.5 1591.3 %reduce-scatter.4.cloned.1.call-start = ((), (), s32[]{:S(2)}) async-start(), calls=%async_computation.7 | async-start | bytes 8421376
  464.3 0.9 copy-start.13
  465.2 1.2 copy-start.5
  465.2 1.4 copy-start.9
  467.5 1.0 copy-start.11
  524.1 1.2 copy-start.12
  540.0 4.2 copy-start.15
Sparse Core Ops, SparseCore 0:
  245.2 89.9 all-gather.1
Sparse Core Ops, SparseCore 1:
  540.1 1509.6 reduce-scatter.3
